TPU v7x, 32 devices: a whole 2x2x4 slice. The times are simulated.
32 devices in a mesh: tiles: 2 (over y), sky: 4 (over x, core), visit: 4 (over z).
Axes of the slice: x: 2, y: 2, z: 4, core: 2. Of those that a mesh axis runs over, the one named last changes fastest.
Arguments:
- sky_model: float32 [512, 4096], P(('tiles', 'sky'), 'visit'), parts along dimension 0, may hold values from -6 to 6
- frames: bfloat16 [16, 128, 2048], P(('tiles', 'visit'), 'sky'), parts along dimension 0, may hold values from -8 to 8
- psf_rows: float32 [16, 5], P('tiles'), parts along dimension 0, may hold values from 0.1 to 1
- psf_cols: float32 [16, 5], P('tiles'), parts along dimension 0, may hold values from 0.1 to 1
- dither: int32 [16, 2], P('tiles'), parts along dimension 0, may hold values from -2 to 2
- footprint: int32 [16, 2], P('tiles'), parts along dimension 0, may hold values from 0 to 128, as said below
- huber_cut: float32 [16], P('tiles'), parts along dimension 0, may hold values from 0.3 to 1.5
Outputs:
- gradient: float32 [512, 4096], P(('tiles', 'sky'), 'visit'), parts along dimension 0
There are 2 independent parts, one for each index of `tiles`. A program takes and returns all parts, laid end to end along the dimension named above; each array names one. Nothing has to cross between parts.
Inputs may be any that keep to these rules, and one draw needn't show every extreme that they name: `footprint`: each row is a visit's first covered frame row and one past its last, the first below the second; some visit starts at row 0 and some ends at row 128.
All inputs are finite; a program needn't handle non-finite values.
Results may differ from a plain program's by a relative error of at most 0.0003.
Values may be sent and summed in bfloat16 or wider, within the bound.
A program may use at most 128 MiB of HBM per device.

v0:
```python
import jax
import jax.numpy as jnp
from jax import lax
from jax.sharding import PartitionSpec as P

TAPS = 5
eps_flux = 0.1
tv_weight = 0.5
dither_bound = 2


def padded_2(value, sides, width):
    for axis, dim in sides:
        count, length = (lax.axis_size(axis), value.shape[dim])
        up = [(i, (i + 1) % count) for i in range(count - 1)]
        down = [(j, i) for i, j in up]
        last = lax.slice_in_dim(value, length - width, length, axis=dim)
        initial = lax.slice_in_dim(value, 0, width, axis=dim)
        before = lax.ppermute(last, axis, up)
        after = lax.ppermute(initial, axis, down)
        value = jnp.concatenate([before, value, after], axis=dim)
    return value


def blur_down(values, offset, kernel, length, along_dim):
    half_taps = TAPS // 2
    margin = half_taps + dither_bound
    accum = None
    for b in range(TAPS):
        begin = offset + (b - half_taps + margin)
        piece = kernel[b] * lax.dynamic_slice_in_dim(values, begin, length, along_dim)
        accum = piece if accum is None else accum + piece
    if along_dim == 0:
        return accum[::2]
    return accum[:, ::2]


def spread_up(small, offset, kernel, extra, along_dim):
    half_taps = TAPS // 2
    margin = half_taps + dither_bound
    blank = jnp.zeros_like(small)
    if along_dim == 0:
        upsampled = jnp.stack([small, blank], 1).reshape(2 * small.shape[0], small.shape[1])
        padding = ((margin + extra, margin + extra), (0, 0))
    else:
        upsampled = jnp.stack([small, blank], 2).reshape(small.shape[0], 2 * small.shape[1])
        padding = ((0, 0), (margin + extra, margin + extra))
    padded = jnp.pad(upsampled, padding)
    length = upsampled.shape[along_dim] + 2 * extra
    accum = None
    for b in range(TAPS):
        begin = margin + half_taps - b - offset
        piece = kernel[b] * lax.dynamic_slice_in_dim(padded, begin, length, along_dim)
        accum = piece if accum is None else accum + piece
    return accum


def flux_divergence(window):
    grad_x = window[1:, :-1] - window[:-1, :-1]
    grad_y = window[:-1, 1:] - window[:-1, :-1]
    magnitude = jnp.sqrt(grad_x * grad_x + grad_y * grad_y + eps_flux)
    flux_u = grad_x / magnitude
    flux_w = grad_y / magnitude
    return flux_u[:-1, 1:] - flux_u[1:, 1:] + (flux_w[1:, :-1] - flux_w[1:, 1:])


def visit_rows(columns, frame, row_shift, kernel, cutoff, first, last, row_start):
    margin = TAPS // 2 + dither_bound
    predicted = blur_down(columns, row_shift, kernel, 2 * frame.shape[0], 0)
    low_index = row_start + jnp.arange(frame.shape[0], dtype=jnp.int32)
    inside = (low_index >= first) & (low_index < last)
    clipped = jnp.where(
        inside[:, None],
        jnp.clip(predicted - frame.astype(jnp.float32), -cutoff, cutoff),
        jnp.zeros_like(predicted),
    )
    return spread_up(clipped, row_shift, kernel, margin, 0)


def fold_rows(summed):
    margin = TAPS // 2 + dither_bound
    edges = jnp.concatenate([summed[:margin], summed[-margin:]], 0)
    arrived = padded_2(edges, (("sky", 0),), margin)
    middle = summed[margin:-margin]
    middle = middle.at[:margin].add(arrived[:margin])
    middle = middle.at[-margin:].add(arrived[-margin:])
    return middle


def on_device(sky_model, frames, psf_rows, psf_cols, dither, footprint, huber_cut):
    margin = TAPS // 2 + dither_bound
    visits = psf_rows.shape[0]
    per_device = frames.shape[0]
    sky_pos = lax.axis_index("sky")
    visit_pos = lax.axis_index("visit")
    row_start = sky_pos * frames.shape[1]
    height = sky_model.shape[0]
    local_width = sky_model.shape[1]
    with_rows = padded_2(sky_model, (("sky", 0),), margin)
    whole = lax.all_gather(with_rows, "visit", axis=1, tiled=True)
    full_width = whole.shape[1]
    padded = jnp.pad(whole, ((0, 0), (margin, margin)))

    def one_visit(j, accum):
        k = visit_pos * per_device + j
        col_shift = dither[k, 1]
        columns = blur_down(padded, col_shift, psf_cols[k], full_width, 1)
        back_rows = visit_rows(
            columns,
            frames[j],
            dither[k, 0],
            psf_rows[k],
            huber_cut[k],
            footprint[k, 0],
            footprint[k, 1],
            row_start,
        )
        return accum + spread_up(back_rows, col_shift, psf_cols[k], 0, 1)

    partial_sum = lax.fori_loop(
        0, per_device, one_visit, jnp.zeros((height + 2 * margin, full_width), jnp.float32)
    )
    summed = lax.psum_scatter(partial_sum, "visit", scatter_dimension=1, tiled=True)
    window = lax.dynamic_slice(
        padded, (margin - 1, visit_pos * local_width + margin - 1), (height + 2, local_width + 2)
    )
    data_term = fold_rows(summed)
    return data_term / jnp.sqrt(jnp.float32(visits)) + tv_weight * flux_divergence(window)


def solution(mesh):
    in_specs = (
        P(("tiles", "sky"), "visit"),
        P(("tiles", "visit"), "sky", None),
        P("tiles", None),
        P("tiles", None),
        P("tiles", None),
        P("tiles", None),
        P("tiles"),
    )
    out_specs = P(("tiles", "sky"), "visit")
    return jax.shard_map(
        on_device, mesh=mesh, in_specs=in_specs, out_specs=out_specs, check_vma=False
    )
```

profile of v0, /device:TPU:1, one launch (start us, length us, event | category | flops | bytes accessed | tf_op | source)
XLA Modules:
  0.0 257.1 jit_solution(7931462190371256638)
XLA Ops:
  7.3 4.5 %collective-permute-start = (f32[4,1024]{1,0:T(4,128)S(1)}, f32[4,1024]{1,0:T(4,128)S(1)}, u32[]{:S(2)}, u32[]{:S(2)}) collective-permute-start(f32[4,1024]{1,0:T(4,128)S(1)} %get-tuple-element.474), channel_id=1, source_target_pairs={{0,4},{4,8},{8,12},{1,5},{5,9},{9,13},{2,6},{6,10},{10,14},{3,7},{... | collective-permute-start | bytes 49160 | tf_op jit(solution)/shard_map/ppermute | solution.py:19
  11.8 1.9 collective-permute-start.1
  13.8 3.1 %collective-permute-done.1 = f32[4,1024]{1,0:T(4,128)S(1)} collective-permute-done((f32[4,1024]{1,0:T(4,128)S(1)}, f32[4,1024]{1,0:T(4,128)S(1)}, u32[]{:S(2)}, u32[]{:S(2)}) %collective-permute-start.1) | collective-permute-done | bytes 16416 | tf_op jit(solution)/shard_map/ppermute | solution.py:20
  16.9 1.7 pad_maximum_fusion
  18.7 29.8 %all-gather.2.cloned.1.call-done = f32[72,4096]{1,0:T(8,128)} async-done(((f32[72,1024]{1,0:T(8,128)}), f32[72,4096]{1,0:T(8,128)}) %all-gather.2.cloned.1.call-update) | async-done | bytes 1179664 | tf_op jit(solution)/shard_map/all_gather | solution.py:100
  48.4 2.7 %copy.16 = f32[72,4096]{0,1:T(8,128)} copy(f32[72,4096]{1,0:T(8,128)} %all-gather.2.cloned.1.call-done) | data formatting | bytes 2359296
  51.2 1.8 pad.45.clone
  53.1 154.4 %while.19 = (s32[]{:T(128)}, f32[72,4096]{0,1:T(8,128)}, s32[]{:T(128)}, f32[8,5]{1,0:T(8,128)}, f32[8,5]{1,0:T(8,128)}, /*index=5*/s32[]{:T(128)}, s32[8,2]{0,1...) while((s32[]{:T(128)}, f32[72,4096]{0,1:T(8,128)}, ...), condition=%wide.region_1.2_spmd.clone, body=%wide.region_0.1_spmd.clone.sunk | while | flops 8732888 | bytes 32507664 | solution.py:120
  83.0 5.7 %multiply_add_fusion.4 = f32[72,4096]{0,1:T(8,128)} fusion(f32[72,4104]{0,1:T(8,128)S(1)} %get-tuple-element.654, s32[]{:T(128)S(6)} %select_n.318, s32[]{:T(128)S(6)} %select_n.319, s32[]{:T(128)S(6)} %select_n.320, s32[]{:T(128)S(6)} %select_n.321, s32[]{:T(128)S(6)} %select_n.322, f32[]{:T(128)} %bitcast.143, f32[]{:T(128)} %bitcast.144, ...), kind=kLoop, calls=%fused_computation.1.clone.1 | loop fusion | flops 2654208 | bytes 7077928 | tf_op jit(solution)/shard_map/while/body/eval_jaxpr/add | solution.py:32
  88.7 5.0 %slice.317 = f32[72,2048]{0,1:T(8,128)S(1)} slice(f32[72,4096]{0,1:T(8,128)} %multiply_add_fusion.4), slice={[0:72:1], [0:4096:2]} | slice | bytes 1179648 | tf_op jit(solution)/shard_map/while/body/eval_jaxpr/slice | solution.py:35
  93.7 5.5 %multiply_add_fusion.5 = f32[64,2048]{0,1:T(8,128)} fusion(f32[72,2048]{0,1:T(8,128)S(1)} %slice.317, s32[]{:T(128)S(6)} %select_n.323, s32[]{:T(128)S(6)} %select_n.324, s32[]{:T(128)S(6)} %select_n.325, s32[]{:T(128)S(6)} %select_n.326, s32[]{:T(128)S(6)} %select_n.327, f32[]{:T(128)} %bitcast.158, f32[]{:T(128)} %bitcast.159, f32[]{:T(128)} %bitcast.160, ...), kind=kLoop, calls=%fused_computation.7.clone.1 | loop fusion | flops 1179648 | bytes 3145768 | tf_op jit(solution)/shard_map/while/body/eval_jaxpr/add | solution.py:32
  99.2 11.0 %slice.318 = f32[32,2048]{0,1:T(8,128)S(1)} slice(f32[64,2048]{0,1:T(8,128)} %multiply_add_fusion.5), slice={[0:64:2], [0:2048:1]} | slice | bytes 524288 | tf_op jit(solution)/shard_map/while/body/eval_jaxpr/slice | solution.py:34
  110.2 2.9 %fusion.31 = f32[32,1,2048]{0,2,1:T(8,128)} fusion(f32[32,2048]{0,1:T(8,128)S(1)} %slice.318, bf16[1,32,2048]{1,2,0:T(8,128)(2,1)} %copy.20, f32[]{:T(128)S(6)} %neg.13, f32[]{:T(128)} %bitcast.163, pred[32]{0:T(512)(128)(4,1)S(1)} %compare_and_fusion.2), kind=kLoop, calls=%fused_computation.6.clone.1 | loop fusion | flops 327680 | bytes 655400 | tf_op jit(solution)/shard_map/while/body/eval_jaxpr/stack | solution.py:43
  113.1 1.6 copy.21
  115.3 4.3 %fusion.32 = f32[72,2048,1]{1,0,2:T(8,128)} fusion(s32[]{:T(128)S(6)} %select_n.317, f32[64,2048]{1,0:T(8,128)S(1)} %reshape.185, s32[]{:T(128)S(6)} %select_n.328, s32[]{:T(128)S(6)} %select_n.329, s32[]{:T(128)S(6)} %select_n.330, s32[]{:T(128)S(6)} %select_n.331, f32[]{:T(128)} %bitcast.158, f32[]{:T(128)} %bitcast.159, f32[]{:T(128)} %bitcast.160, ...), kind=kLoop, calls=%fused_computation.18.clone.1 | loop fusion | flops 1327104 | bytes 1114152 | tf_op jit(solution)/shard_map/while/body/eval_jaxpr/stack | solution.py:46
  119.6 2.2 copy.22
  123.5 5.4 %select_add_fusion.2 = f32[72,4096]{0,1:T(8,128)S(1)} fusion(f32[72,4096]{0,1:T(8,128)S(1)} %copy-done, s32[]{:T(128)S(6)} %select_n.312, s32[]{:T(128)S(6)} %select_n.313, s32[]{:T(128)S(6)} %select_n.314, s32[]{:T(128)S(6)} %select_n.315, s32[]{:T(128)S(6)} %select_n.316, f32[72,4096]{0,1:T(8,128)S(1)} %bitcast.175, f32[]{:T(128)} %bitcast.143, ...), kind=kLoop, calls=%fused_computation.clone.1 | loop fusion | flops 3244032 | bytes 3538985 | tf_op jit(solution)/shard_map/while/body/eval_jaxpr/add | solution.py:118
  128.9 1.3 copy-done.1
  160.1 5.7 %multiply_add_fusion.4 = f32[72,4096]{0,1:T(8,128)} fusion(f32[72,4104]{0,1:T(8,128)S(1)} %get-tuple-element.654, s32[]{:T(128)S(6)} %select_n.318, s32[]{:T(128)S(6)} %select_n.319, s32[]{:T(128)S(6)} %select_n.320, s32[]{:T(128)S(6)} %select_n.321, s32[]{:T(128)S(6)} %select_n.322, f32[]{:T(128)} %bitcast.143, f32[]{:T(128)} %bitcast.144, ...), kind=kLoop, calls=%fused_computation.1.clone.1 | loop fusion | flops 2654208 | bytes 7077928 | tf_op jit(solution)/shard_map/while/body/eval_jaxpr/add | solution.py:32
  165.9 5.0 %slice.317 = f32[72,2048]{0,1:T(8,128)S(1)} slice(f32[72,4096]{0,1:T(8,128)} %multiply_add_fusion.4), slice={[0:72:1], [0:4096:2]} | slice | bytes 1179648 | tf_op jit(solution)/shard_map/while/body/eval_jaxpr/slice | solution.py:35
  170.9 5.5 %multiply_add_fusion.5 = f32[64,2048]{0,1:T(8,128)} fusion(f32[72,2048]{0,1:T(8,128)S(1)} %slice.317, s32[]{:T(128)S(6)} %select_n.323, s32[]{:T(128)S(6)} %select_n.324, s32[]{:T(128)S(6)} %select_n.325, s32[]{:T(128)S(6)} %select_n.326, s32[]{:T(128)S(6)} %select_n.327, f32[]{:T(128)} %bitcast.158, f32[]{:T(128)} %bitcast.159, f32[]{:T(128)} %bitcast.160, ...), kind=kLoop, calls=%fused_computation.7.clone.1 | loop fusion | flops 1179648 | bytes 3145768 | tf_op jit(solution)/shard_map/while/body/eval_jaxpr/add | solution.py:32
  176.4 11.0 %slice.318 = f32[32,2048]{0,1:T(8,128)S(1)} slice(f32[64,2048]{0,1:T(8,128)} %multiply_add_fusion.5), slice={[0:64:2], [0:2048:1]} | slice | bytes 524288 | tf_op jit(solution)/shard_map/while/body/eval_jaxpr/slice | solution.py:34
  187.4 2.9 %fusion.31 = f32[32,1,2048]{0,2,1:T(8,128)} fusion(f32[32,2048]{0,1:T(8,128)S(1)} %slice.318, bf16[1,32,2048]{1,2,0:T(8,128)(2,1)} %copy.20, f32[]{:T(128)S(6)} %neg.13, f32[]{:T(128)} %bitcast.163, pred[32]{0:T(512)(128)(4,1)S(1)} %compare_and_fusion.2), kind=kLoop, calls=%fused_computation.6.clone.1 | loop fusion | flops 327680 | bytes 655400 | tf_op jit(solution)/shard_map/while/body/eval_jaxpr/stack | solution.py:43
  190.3 1.6 copy.21
  192.5 4.3 %fusion.32 = f32[72,2048,1]{1,0,2:T(8,128)} fusion(s32[]{:T(128)S(6)} %select_n.317, f32[64,2048]{1,0:T(8,128)S(1)} %reshape.185, s32[]{:T(128)S(6)} %select_n.328, s32[]{:T(128)S(6)} %select_n.329, s32[]{:T(128)S(6)} %select_n.330, s32[]{:T(128)S(6)} %select_n.331, f32[]{:T(128)} %bitcast.158, f32[]{:T(128)} %bitcast.159, f32[]{:T(128)} %bitcast.160, ...), kind=kLoop, calls=%fused_computation.18.clone.1 | loop fusion | flops 1327104 | bytes 1114152 | tf_op jit(solution)/shard_map/while/body/eval_jaxpr/stack | solution.py:46
  196.8 2.2 copy.22
  200.7 5.4 %select_add_fusion.2 = f32[72,4096]{0,1:T(8,128)S(1)} fusion(f32[72,4096]{0,1:T(8,128)S(1)} %copy-done, s32[]{:T(128)S(6)} %select_n.312, s32[]{:T(128)S(6)} %select_n.313, s32[]{:T(128)S(6)} %select_n.314, s32[]{:T(128)S(6)} %select_n.315, s32[]{:T(128)S(6)} %select_n.316, f32[72,4096]{0,1:T(8,128)S(1)} %bitcast.175, f32[]{:T(128)} %bitcast.143, ...), kind=kLoop, calls=%fused_computation.clone.1 | loop fusion | flops 3244032 | bytes 3538985 | tf_op jit(solution)/shard_map/while/body/eval_jaxpr/add | solution.py:118
  207.4 2.8 %copy.12 = f32[72,4096]{1,0:T(8,128)} copy(f32[72,4096]{0,1:T(8,128)} %get-tuple-element.382) | data formatting | bytes 2359296 | tf_op jit(solution)/shard_map/while | solution.py:120
  210.3 28.7 %reduce-scatter.2.cloned.1.call-done = f32[72,1024]{1,0:T(8,128)} async-done(((f32[72,4096]{1,0:T(8,128)}), f32[72,1024]{1,0:T(8,128)}) %reduce-scatter.2.cloned.1.call-update) | async-done | bytes 294928 | tf_op jit(solution)/shard_map/reduce_scatter | solution.py:123
  239.8 3.8 %collective-permute-start.2 = (f32[4,1024]{1,0:T(4,128)S(1)}, f32[4,1024]{1,0:T(4,128)S(1)}, u32[]{:S(2)}, u32[]{:S(2)}) collective-permute-start(f32[4,1024]{1,0:T(4,128)S(1)} %get-tuple-element.473), channel_id=1, source_target_pairs={{0,4},{4,8},{8,12},{1,5},{5,9},{9,13},{2,6},{6,10},{10,14},{3,7},{... | collective-permute-start | bytes 49160 | tf_op jit(solution)/shard_map/ppermute | solution.py:19
  244.2 1.9 collective-permute-start.3
  247.9 1.4 collective-permute-done.3
  (53 shorter events, 22.0 us)
Async XLA Ops:
  6.5 41.9 %all-gather.2.cloned.1.call-start = ((), (), s32[]{:S(2)}) async-start(), calls=%async_computation.1 | async-start | bytes 1474560 | tf_op jit(solution)/shard_map/all_gather | solution.py:100
  7.3 6.4 %collective-permute-start = (f32[4,1024]{1,0:T(4,128)S(1)}, f32[4,1024]{1,0:T(4,128)S(1)}, u32[]{:S(2)}, u32[]{:S(2)}) collective-permute-start(f32[4,1024]{1,0:T(4,128)S(1)} %get-tuple-element.474), channel_id=1, source_target_pairs={{0,4},{4,8},{8,12},{1,5},{5,9},{9,13},{2,6},{6,10},{10,14},{3,7},{... | collective-permute-start | bytes 49160 | tf_op jit(solution)/shard_map/ppermute | solution.py:19
  11.8 5.1 %collective-permute-start.1 = (f32[4,1024]{1,0:T(4,128)S(1)}, f32[4,1024]{1,0:T(4,128)S(1)}, u32[]{:S(2)}, u32[]{:S(2)}) collective-permute-start(f32[4,1024]{1,0:T(4,128)S(1)} %get-tuple-element.475), channel_id=1, source_target_pairs={{4,0},{8,4},{12,8},{5,1},{9,5},{13,9},{6,2},{10,6},{14,10},{7,3},{... | collective-permute-start | bytes 49160 | tf_op jit(solution)/shard_map/ppermute | solution.py:20
  18.6 220.4 %reduce-scatter.2.cloned.1.call-start = ((), (), s32[]{:S(2)}) async-start(), calls=%async_computation.2 | async-start | bytes 1474560 | tf_op jit(solution)/shard_map/reduce_scatter | solution.py:123
  51.2 1.9 copy-start.3
  51.2 1.9 copy-start.4
  51.2 1.9 copy-start.5
  51.2 1.9 copy-start.6
  121.9 1.6 copy-start
  128.9 1.3 copy-start.1
  199.1 1.6 copy-start
  206.1 1.3 copy-start.1
  207.4 36.2 %copy-start.2 = (f32[72,4096]{1,0:T(8,128)S(1)}, f32[72,4096]{1,0:T(8,128)}, u32[]{:S(2)}) copy-start(f32[72,4096]{1,0:T(8,128)} %all-gather.2.cloned.1.call-done) | copy-start | bytes 3538948
  239.8 7.4 %collective-permute-start.2 = (f32[4,1024]{1,0:T(4,128)S(1)}, f32[4,1024]{1,0:T(4,128)S(1)}, u32[]{:S(2)}, u32[]{:S(2)}) collective-permute-start(f32[4,1024]{1,0:T(4,128)S(1)} %get-tuple-element.473), channel_id=1, source_target_pairs={{0,4},{4,8},{8,12},{1,5},{5,9},{9,13},{2,6},{6,10},{10,14},{3,7},{... | collective-permute-start | bytes 49160 | tf_op jit(solution)/shard_map/ppermute | solution.py:19
  244.2 5.1 %collective-permute-start.3 = (f32[4,1024]{1,0:T(4,128)S(1)}, f32[4,1024]{1,0:T(4,128)S(1)}, u32[]{:S(2)}, u32[]{:S(2)}) collective-permute-start(f32[4,1024]{1,0:T(4,128)S(1)} %get-tuple-element.472), channel_id=1, source_target_pairs={{4,0},{8,4},{12,8},{5,1},{9,5},{13,9},{6,2},{10,6},{14,10},{7,3},{... | collective-permute-start | bytes 49160 | tf_op jit(solution)/shard_map/ppermute | solution.py:20
Sparse Core Ops, SparseCore 0:
  18.7 29.6 all-gather.1
  210.4 28.5 reduce-scatter.1
where the time goes:
time: 259 us; the launch traced here: 257 us
  local copies, waits for them, and re-layouts  65.4 us (25%)
  waiting for transfers between devices  63 us (24%)
  other arithmetic  54.3 us (21%)
  loops' own time  48.8 us (19%)
  between operations  13.5 us (5%)
  starting transfers between devices  12.2 us (5%)
    another operation x1, loops' own time, on_device(): lax.fori_loop(0, per_device, one_visit, jnp.zeros((height + 2 * margin, f...  48.8 us
    all_gather x1, waiting for transfers between devices, on_device(): whole = lax.all_gather(with_rows, 'visit', axis=1, tiled=True)  29.8 us
    reduce_scatter x1, waiting for transfers between devices, on_device(): lax.psum_scatter(partial_sum, 'visit', scatter_dimension=1, tiled=True)  28.7 us
    add x4, other arithmetic, blur_down(): accum = piece if accum is None else accum + piece  22.4 us
    slice x2, local copies, waits for them, and re-layouts, blur_down(): return accum[::2]  22.1 us
    while x12, local copies, waits for them, and re-layouts  11.8 us
    add x2, other arithmetic, one_visit(): return accum + spread_up(back_rows, col_shift, psf_cols[k], 0, 1)  10.9 us
    slice x2, local copies, waits for them, and re-layouts, blur_down(): return accum[:, ::2]  10 us
  transfers between devices with their start and end apart: 6, of which 4 were waited for; matrix products, arithmetic and copies ran while one was open for 1% of the time, Pallas kernels for 0%

commit v1 on v0

--- a/solution.py
+++ b/solution.py
@@ -97,7 +97,14 @@
     height = sky_model.shape[0]
     local_width = sky_model.shape[1]
     with_rows = padded_2(sky_model, (("sky", 0),), margin)
-    whole = lax.all_gather(with_rows, "visit", axis=1, tiled=True)
+    ring = [with_rows]
+    for hop in range(3):
+        ring.append(lax.ppermute(ring[-1], "visit", [(dev, (dev + 1) % 4) for dev in range(4)]))
+    whole = jnp.roll(
+        jnp.concatenate(ring[::-1], axis=1),
+        (lax.axis_index("visit") + 1) * ring[0].shape[1],
+        axis=1,
+    )
     full_width = whole.shape[1]
     padded = jnp.pad(whole, ((0, 0), (margin, margin)))
 

time: 259 us -> 257 us (level)
  waiting for transfers between devices: 63 us -> 59.3 us
    all_gather x1 -> x0, waiting for transfers between devices: 29.8 us -> none  [on_device(): whole = lax.all_gather(with_rows, 'visit', axis=1, tiled=True)]
    ppermute x0 -> x3, waiting for transfers between devices: none -> 27.9 us  [on_device(): lax.ppermute(ring[-1], 'visit', [(dev, (dev + 1) % 4) for dev in range(4)])]
  transfers between devices with their start and end apart: 6 -> 8, of which waited for: 4 -> 6; matrix products, arithmetic and copies ran while one was open for 1% -> 1% of each run, Pallas kernels for 0% -> 0%
where the time goes in v1:
time: 257 us; the launch traced here: 255 us
  local copies, waits for them, and re-layouts  65.8 us (26%)
  waiting for transfers between devices  59.3 us (23%)
  other arithmetic  53.5 us (21%)
  loops' own time  49.6 us (19%)
  between operations  13.6 us (5%)
  starting transfers between devices  13.5 us (5%)
    another operation x1, loops' own time, on_device(): lax.fori_loop(0, per_device, one_visit, jnp.zeros((height + 2 * margin, f...  49.6 us
    ppermute x3, waiting for transfers between devices, on_device(): lax.ppermute(ring[-1], 'visit', [(dev, (dev + 1) % 4) for dev in range(4)])  27.9 us
    reduce_scatter x1, waiting for transfers between devices, on_device(): lax.psum_scatter(partial_sum, 'visit', scatter_dimension=1, tiled=True)  26.9 us
    add x4, other arithmetic, blur_down(): accum = piece if accum is None else accum + piece  22.4 us
    slice x2, local copies, waits for them, and re-layouts, blur_down(): return accum[::2]  22.1 us
    while x12, local copies, waits for them, and re-layouts  11.9 us
    add x2, other arithmetic, one_visit(): return accum + spread_up(back_rows, col_shift, psf_cols[k], 0, 1)  10.7 us
    slice x2, local copies, waits for them, and re-layouts, blur_down(): return accum[:, ::2]  10 us
  transfers between devices with their start and end apart: 8, of which 6 were waited for; matrix products, arithmetic and copies ran while one was open for 1% of the time, Pallas kernels for 0%

profile of v1, /device:TPU:1, one launch (start us, length us, event | category | flops | bytes accessed | tf_op | source)
XLA Modules:
  0.0 255.3 jit_solution(5614754294865582333)
XLA Ops:
  7.4 4.5 %collective-permute-start = (f32[4,1024]{1,0:T(4,128)S(1)}, f32[4,1024]{1,0:T(4,128)S(1)}, u32[]{:S(2)}, u32[]{:S(2)}) collective-permute-start(f32[4,1024]{1,0:T(4,128)S(1)} %get-tuple-element.474), channel_id=1, source_target_pairs={{0,4},{4,8},{8,12},{1,5},{5,9},{9,13},{2,6},{6,10},{10,14},{3,7},{... | collective-permute-start | bytes 49160 | tf_op jit(solution)/shard_map/ppermute | solution.py:19
  11.9 1.9 collective-permute-start.1
  13.8 3.1 %collective-permute-done.1 = f32[4,1024]{1,0:T(4,128)S(1)} collective-permute-done((f32[4,1024]{1,0:T(4,128)S(1)}, f32[4,1024]{1,0:T(4,128)S(1)}, u32[]{:S(2)}, u32[]{:S(2)}) %collective-permute-start.1) | collective-permute-done | bytes 16416 | tf_op jit(solution)/shard_map/ppermute | solution.py:20
  19.3 7.7 %collective-permute-done.2 = f32[72,1024]{1,0:T(8,128)S(1)} collective-permute-done((f32[72,1024]{1,0:T(8,128)S(1)}, f32[72,1024]{1,0:T(8,128)S(1)}, u32[]{:S(2)}, u32[]{:S(2)}) %collective-permute-start.2) | collective-permute-done | bytes 294944 | tf_op jit(solution)/shard_map/ppermute | solution.py:102
  27.0 10.0 %collective-permute-done.3 = f32[72,1024]{1,0:T(8,128)S(1)} collective-permute-done((f32[72,1024]{1,0:T(8,128)S(1)}, f32[72,1024]{1,0:T(8,128)S(1)}, u32[]{:S(2)}, u32[]{:S(2)}) %collective-permute-start.3) | collective-permute-done | bytes 294944 | tf_op jit(solution)/shard_map/ppermute | solution.py:102
  37.0 10.1 %collective-permute-done.4 = f32[72,1024]{1,0:T(8,128)S(1)} collective-permute-done((f32[72,1024]{1,0:T(8,128)S(1)}, f32[72,1024]{1,0:T(8,128)S(1)}, u32[]{:S(2)}, u32[]{:S(2)}) %collective-permute-start.4) | collective-permute-done | bytes 294944 | tf_op jit(solution)/shard_map/ppermute | solution.py:102
  48.6 1.8 copy.16
  50.4 1.8 pad.45.clone
  52.2 155.2 %while.19 = (s32[]{:T(128)}, f32[72,4096]{0,1:T(8,128)}, s32[]{:T(128)}, f32[8,5]{1,0:T(8,128)}, f32[8,5]{1,0:T(8,128)}, /*index=5*/s32[]{:T(128)}, s32[8,2]{0,1...) while((s32[]{:T(128)}, f32[72,4096]{0,1:T(8,128)}, ...), condition=%wide.region_1.2_spmd.clone, body=%wide.region_0.1_spmd.clone.sunk | while | flops 8732888 | bytes 32507664 | solution.py:127
  82.5 5.7 %multiply_add_fusion.4 = f32[72,4096]{0,1:T(8,128)} fusion(f32[72,4104]{0,1:T(8,128)S(1)} %get-tuple-element.654, s32[]{:T(128)S(6)} %select_n.333, s32[]{:T(128)S(6)} %select_n.334, s32[]{:T(128)S(6)} %select_n.335, s32[]{:T(128)S(6)} %select_n.336, s32[]{:T(128)S(6)} %select_n.337, f32[]{:T(128)} %bitcast.143, f32[]{:T(128)} %bitcast.144, ...), kind=kLoop, calls=%fused_computation.1.clone.1 | loop fusion | flops 2654208 | bytes 7077928 | tf_op jit(solution)/shard_map/while/body/eval_jaxpr/add | solution.py:32
  88.2 5.0 %slice.317 = f32[72,2048]{0,1:T(8,128)S(1)} slice(f32[72,4096]{0,1:T(8,128)} %multiply_add_fusion.4), slice={[0:72:1], [0:4096:2]} | slice | bytes 1179648 | tf_op jit(solution)/shard_map/while/body/eval_jaxpr/slice | solution.py:35
  93.2 5.6 %multiply_add_fusion.5 = f32[64,2048]{0,1:T(8,128)} fusion(f32[72,2048]{0,1:T(8,128)S(1)} %slice.317, s32[]{:T(128)S(6)} %select_n.338, s32[]{:T(128)S(6)} %select_n.339, s32[]{:T(128)S(6)} %select_n.340, s32[]{:T(128)S(6)} %select_n.341, s32[]{:T(128)S(6)} %select_n.342, f32[]{:T(128)} %bitcast.158, f32[]{:T(128)} %bitcast.159, f32[]{:T(128)} %bitcast.160, ...), kind=kLoop, calls=%fused_computation.7.clone.1 | loop fusion | flops 1179648 | bytes 3145768 | tf_op jit(solution)/shard_map/while/body/eval_jaxpr/add | solution.py:32
  98.8 11.0 %slice.318 = f32[32,2048]{0,1:T(8,128)S(1)} slice(f32[64,2048]{0,1:T(8,128)} %multiply_add_fusion.5), slice={[0:64:2], [0:2048:1]} | slice | bytes 524288 | tf_op jit(solution)/shard_map/while/body/eval_jaxpr/slice | solution.py:34
  109.8 2.9 %fusion.31 = f32[32,1,2048]{0,2,1:T(8,128)} fusion(f32[32,2048]{0,1:T(8,128)S(1)} %slice.318, bf16[1,32,2048]{1,2,0:T(8,128)(2,1)} %copy.20, f32[]{:T(128)S(6)} %neg.13, f32[]{:T(128)} %bitcast.163, pred[32]{0:T(512)(128)(4,1)S(1)} %compare_and_fusion.2), kind=kLoop, calls=%fused_computation.6.clone.1 | loop fusion | flops 327680 | bytes 655400 | tf_op jit(solution)/shard_map/while/body/eval_jaxpr/stack | solution.py:43
  112.7 1.6 copy.21
  114.9 4.4 %fusion.32 = f32[72,2048,1]{1,0,2:T(8,128)} fusion(s32[]{:T(128)S(6)} %select_n.332, f32[64,2048]{1,0:T(8,128)S(1)} %reshape.185, s32[]{:T(128)S(6)} %select_n.343, s32[]{:T(128)S(6)} %select_n.344, s32[]{:T(128)S(6)} %select_n.345, s32[]{:T(128)S(6)} %select_n.346, f32[]{:T(128)} %bitcast.158, f32[]{:T(128)} %bitcast.159, f32[]{:T(128)} %bitcast.160, ...), kind=kLoop, calls=%fused_computation.18.clone.1 | loop fusion | flops 1327104 | bytes 1114152 | tf_op jit(solution)/shard_map/while/body/eval_jaxpr/stack | solution.py:46
  119.3 2.2 copy.22
  123.2 5.3 %select_add_fusion.2 = f32[72,4096]{0,1:T(8,128)S(1)} fusion(f32[72,4096]{0,1:T(8,128)S(1)} %copy-done, s32[]{:T(128)S(6)} %select_n.327, s32[]{:T(128)S(6)} %select_n.328, s32[]{:T(128)S(6)} %select_n.329, s32[]{:T(128)S(6)} %select_n.330, s32[]{:T(128)S(6)} %select_n.331, f32[72,4096]{0,1:T(8,128)S(1)} %bitcast.175, f32[]{:T(128)} %bitcast.143, ...), kind=kLoop, calls=%fused_computation.clone.1 | loop fusion | flops 3244032 | bytes 3538985 | tf_op jit(solution)/shard_map/while/body/eval_jaxpr/add | solution.py:125
  160.1 5.7 %multiply_add_fusion.4 = f32[72,4096]{0,1:T(8,128)} fusion(f32[72,4104]{0,1:T(8,128)S(1)} %get-tuple-element.654, s32[]{:T(128)S(6)} %select_n.333, s32[]{:T(128)S(6)} %select_n.334, s32[]{:T(128)S(6)} %select_n.335, s32[]{:T(128)S(6)} %select_n.336, s32[]{:T(128)S(6)} %select_n.337, f32[]{:T(128)} %bitcast.143, f32[]{:T(128)} %bitcast.144, ...), kind=kLoop, calls=%fused_computation.1.clone.1 | loop fusion | flops 2654208 | bytes 7077928 | tf_op jit(solution)/shard_map/while/body/eval_jaxpr/add | solution.py:32
  165.8 5.0 %slice.317 = f32[72,2048]{0,1:T(8,128)S(1)} slice(f32[72,4096]{0,1:T(8,128)} %multiply_add_fusion.4), slice={[0:72:1], [0:4096:2]} | slice | bytes 1179648 | tf_op jit(solution)/shard_map/while/body/eval_jaxpr/slice | solution.py:35
  170.8 5.6 %multiply_add_fusion.5 = f32[64,2048]{0,1:T(8,128)} fusion(f32[72,2048]{0,1:T(8,128)S(1)} %slice.317, s32[]{:T(128)S(6)} %select_n.338, s32[]{:T(128)S(6)} %select_n.339, s32[]{:T(128)S(6)} %select_n.340, s32[]{:T(128)S(6)} %select_n.341, s32[]{:T(128)S(6)} %select_n.342, f32[]{:T(128)} %bitcast.158, f32[]{:T(128)} %bitcast.159, f32[]{:T(128)} %bitcast.160, ...), kind=kLoop, calls=%fused_computation.7.clone.1 | loop fusion | flops 1179648 | bytes 3145768 | tf_op jit(solution)/shard_map/while/body/eval_jaxpr/add | solution.py:32
  176.3 11.0 %slice.318 = f32[32,2048]{0,1:T(8,128)S(1)} slice(f32[64,2048]{0,1:T(8,128)} %multiply_add_fusion.5), slice={[0:64:2], [0:2048:1]} | slice | bytes 524288 | tf_op jit(solution)/shard_map/while/body/eval_jaxpr/slice | solution.py:34
  187.4 2.9 %fusion.31 = f32[32,1,2048]{0,2,1:T(8,128)} fusion(f32[32,2048]{0,1:T(8,128)S(1)} %slice.318, bf16[1,32,2048]{1,2,0:T(8,128)(2,1)} %copy.20, f32[]{:T(128)S(6)} %neg.13, f32[]{:T(128)} %bitcast.163, pred[32]{0:T(512)(128)(4,1)S(1)} %compare_and_fusion.2), kind=kLoop, calls=%fused_computation.6.clone.1 | loop fusion | flops 327680 | bytes 655400 | tf_op jit(solution)/shard_map/while/body/eval_jaxpr/stack | solution.py:43
  190.3 1.6 copy.21
  192.5 4.4 %fusion.32 = f32[72,2048,1]{1,0,2:T(8,128)} fusion(s32[]{:T(128)S(6)} %select_n.332, f32[64,2048]{1,0:T(8,128)S(1)} %reshape.185, s32[]{:T(128)S(6)} %select_n.343, s32[]{:T(128)S(6)} %select_n.344, s32[]{:T(128)S(6)} %select_n.345, s32[]{:T(128)S(6)} %select_n.346, f32[]{:T(128)} %bitcast.158, f32[]{:T(128)} %bitcast.159, f32[]{:T(128)} %bitcast.160, ...), kind=kLoop, calls=%fused_computation.18.clone.1 | loop fusion | flops 1327104 | bytes 1114152 | tf_op jit(solution)/shard_map/while/body/eval_jaxpr/stack | solution.py:46
  196.9 2.2 copy.22
  200.7 5.3 %select_add_fusion.2 = f32[72,4096]{0,1:T(8,128)S(1)} fusion(f32[72,4096]{0,1:T(8,128)S(1)} %copy-done, s32[]{:T(128)S(6)} %select_n.327, s32[]{:T(128)S(6)} %select_n.328, s32[]{:T(128)S(6)} %select_n.329, s32[]{:T(128)S(6)} %select_n.330, s32[]{:T(128)S(6)} %select_n.331, f32[72,4096]{0,1:T(8,128)S(1)} %bitcast.175, f32[]{:T(128)} %bitcast.143, ...), kind=kLoop, calls=%fused_computation.clone.1 | loop fusion | flops 3244032 | bytes 3538985 | tf_op jit(solution)/shard_map/while/body/eval_jaxpr/add | solution.py:125
  207.4 2.8 %copy.12 = f32[72,4096]{1,0:T(8,128)} copy(f32[72,4096]{0,1:T(8,128)} %get-tuple-element.382) | data formatting | bytes 2359296 | tf_op jit(solution)/shard_map/while | solution.py:127
  210.3 26.9 %reduce-scatter.2.cloned.1.call-done = f32[72,1024]{1,0:T(8,128)} async-done(((f32[72,4096]{1,0:T(8,128)}), f32[72,1024]{1,0:T(8,128)}) %reduce-scatter.2.cloned.1.call-update) | async-done | bytes 294928 | tf_op jit(solution)/shard_map/reduce_scatter | solution.py:130
  237.9 3.8 %collective-permute-start.5 = (f32[4,1024]{1,0:T(4,128)S(1)}, f32[4,1024]{1,0:T(4,128)S(1)}, u32[]{:S(2)}, u32[]{:S(2)}) collective-permute-start(f32[4,1024]{1,0:T(4,128)S(1)} %get-tuple-element.473), channel_id=1, source_target_pairs={{0,4},{4,8},{8,12},{1,5},{5,9},{9,13},{2,6},{6,10},{10,14},{3,7},{... | collective-permute-start | bytes 49160 | tf_op jit(solution)/shard_map/ppermute | solution.py:19
  242.4 1.9 collective-permute-start.6
  246.1 1.4 collective-permute-done.6
  (69 shorter events, 26.8 us)
Async XLA Ops:
  6.5 40.7 %copy-start.4 = (f32[64,1024]{1,0:T(8,128)S(1)}, f32[64,1024]{1,0:T(8,128)}, u32[]{:S(2)}) copy-start(f32[64,1024]{1,0:T(8,128)} %param.13) | copy-start | bytes 786436
  6.5 230.6 %reduce-scatter.2.cloned.1.call-start = ((), (), s32[]{:S(2)}) async-start(), calls=%async_computation.1 | async-start | bytes 1474560 | tf_op jit(solution)/shard_map/reduce_scatter | solution.py:130
  7.4 6.4 %collective-permute-start = (f32[4,1024]{1,0:T(4,128)S(1)}, f32[4,1024]{1,0:T(4,128)S(1)}, u32[]{:S(2)}, u32[]{:S(2)}) collective-permute-start(f32[4,1024]{1,0:T(4,128)S(1)} %get-tuple-element.474), channel_id=1, source_target_pairs={{0,4},{4,8},{8,12},{1,5},{5,9},{9,13},{2,6},{6,10},{10,14},{3,7},{... | collective-permute-start | bytes 49160 | tf_op jit(solution)/shard_map/ppermute | solution.py:19
  11.9 5.1 %collective-permute-start.1 = (f32[4,1024]{1,0:T(4,128)S(1)}, f32[4,1024]{1,0:T(4,128)S(1)}, u32[]{:S(2)}, u32[]{:S(2)}) collective-permute-start(f32[4,1024]{1,0:T(4,128)S(1)} %get-tuple-element.475), channel_id=1, source_target_pairs={{4,0},{8,4},{12,8},{5,1},{9,5},{13,9},{6,2},{10,6},{14,10},{7,3},{... | collective-permute-start | bytes 49160 | tf_op jit(solution)/shard_map/ppermute | solution.py:20
  17.9 9.1 %collective-permute-start.2 = (f32[72,1024]{1,0:T(8,128)S(1)}, f32[72,1024]{1,0:T(8,128)S(1)}, u32[]{:S(2)}, u32[]{:S(2)}) collective-permute-start(f32[72,1024]{1,0:T(8,128)S(1)} %pad_maximum_fusion), channel_id=1, source_target_pairs={{0,1},{1,2},{2,3},{3,0},{4,5},{5,6},{6,7},{7,4},{8,9},{9,10},{10,1... | collective-permute-start | bytes 884744 | tf_op jit(solution)/shard_map/ppermute | solution.py:102
  27.0 10.0 %collective-permute-start.3 = (f32[72,1024]{1,0:T(8,128)S(1)}, f32[72,1024]{1,0:T(8,128)S(1)}, u32[]{:S(2)}, u32[]{:S(2)}) collective-permute-start(f32[72,1024]{1,0:T(8,128)S(1)} %collective-permute-done.2), channel_id=1, source_target_pairs={{0,1},{1,2},{2,3},{3,0},{4,5},{5,6},{6,7},{7,4},{8,9},{9,10},{10,1... | collective-permute-start | bytes 884744 | tf_op jit(solution)/shard_map/ppermute | solution.py:102
  37.0 10.1 %collective-permute-start.4 = (f32[72,1024]{1,0:T(8,128)S(1)}, f32[72,1024]{1,0:T(8,128)S(1)}, u32[]{:S(2)}, u32[]{:S(2)}) collective-permute-start(f32[72,1024]{1,0:T(8,128)S(1)} %collective-permute-done.3), channel_id=1, source_target_pairs={{0,1},{1,2},{2,3},{3,0},{4,5},{5,6},{6,7},{7,4},{8,9},{9,10},{10,1... | collective-permute-start | bytes 884744 | tf_op jit(solution)/shard_map/ppermute | solution.py:102
  47.5 1.1 copy-start.2
  50.3 1.9 copy-start.5
  50.3 1.9 copy-start.6
  50.4 1.9 copy-start.7
  50.4 1.9 copy-start.8
  121.6 1.6 copy-start
  128.5 1.3 copy-start.1
  199.1 1.6 copy-start
  206.1 1.3 copy-start.1
  207.4 34.3 %copy-start.3 = (f32[72,4096]{1,0:T(8,128)S(1)}, f32[72,4096]{1,0:T(8,128)}, u32[]{:S(2)}) copy-start(f32[72,4096]{1,0:T(8,128)} %copy-done.2) | copy-start | bytes 3538948
  237.9 7.4 %collective-permute-start.5 = (f32[4,1024]{1,0:T(4,128)S(1)}, f32[4,1024]{1,0:T(4,128)S(1)}, u32[]{:S(2)}, u32[]{:S(2)}) collective-permute-start(f32[4,1024]{1,0:T(4,128)S(1)} %get-tuple-element.473), channel_id=1, source_target_pairs={{0,4},{4,8},{8,12},{1,5},{5,9},{9,13},{2,6},{6,10},{10,14},{3,7},{... | collective-permute-start | bytes 49160 | tf_op jit(solution)/shard_map/ppermute | solution.py:19
  242.4 5.1 %collective-permute-start.6 = (f32[4,1024]{1,0:T(4,128)S(1)}, f32[4,1024]{1,0:T(4,128)S(1)}, u32[]{:S(2)}, u32[]{:S(2)}) collective-permute-start(f32[4,1024]{1,0:T(4,128)S(1)} %get-tuple-element.472), channel_id=1, source_target_pairs={{4,0},{8,4},{12,8},{5,1},{9,5},{13,9},{6,2},{10,6},{14,10},{7,3},{... | collective-permute-start | bytes 49160 | tf_op jit(solution)/shard_map/ppermute | solution.py:20
Sparse Core Ops, SparseCore 0:
  210.4 26.7 reduce-scatter.1
